TPU v7x, 512 devices: a whole 4x4x16 slice. The times are simulated.
512 devices in a mesh: prow: 16 (over x, y), pcol: 32 (over z, core).
Axes of the slice: x: 4, y: 4, z: 16, core: 2. Of those that a mesh axis runs over, the one named last changes fastest.
Arguments:
- adjoint_trail: float32 [2, 16, 256, 1, 32, 256], P(None, 'prow', None, None, 'pcol'), as said below
- factor_low: float32 [2, 16, 32, 8, 4, 256], P(None, 'prow', 'pcol'), may hold values from -0.0625 to 0.0625
- adjoint_low: float32 [2, 16, 32, 8, 4, 256], P(None, 'prow', 'pcol'), may hold values from -6 to 6
- factor_top: float32 [10, 256, 256], P(None, 'pcol'), as said below
- adjoint_top: float32 [10, 256, 256], P(None, 'pcol'), may hold values from -6 to 6
- diag_inverse: float32 [4, 256, 256], P(None, 'pcol'), as said below
Outputs:
- grad_low: float32 [2, 16, 32, 8, 4, 256], P(None, 'prow', 'pcol')
- grad_top: float32 [10, 256, 256], P(None, 'pcol')
Inputs may be any that keep to these rules, and one draw needn't show every extreme that they name: adjoint_trail reshaped row-major to 8192 x 8192 is symmetric. The diagonal blocks factor_top[j (j + 1) / 2 + j] are lower triangular with a positive diagonal. diag_inverse[j] is the inverse of factor_top[j (j + 1) / 2 + j].
All inputs are finite; a program needn't handle non-finite values.
Results may differ from a plain program's by a relative error of at most 0.00024.
Values sent between devices are 32-bit elements; how exact they have to be, the bound alone decides.
A program may use at most 64 MiB of HBM per device.

v0:
```python
import jax
import jax.numpy as jnp
from jax import lax
from jax.sharding import PartitionSpec as P

NB = 256
K = 4
HIGHEST = lax.Precision.HIGHEST


def from_root(array, axis, root):
    mine = lax.axis_index(axis) == root
    return lax.psum(jnp.where(mine, array, jnp.zeros_like(array)), axis)


def matmul(left, right):
    return jnp.dot(left, right, precision=HIGHEST, preferred_element_type=jnp.float32)


def inner_product(left, right):
    return lax.dot_general(
        left, right, (((0,), (0,)), ((), ())), precision=HIGHEST, preferred_element_type=jnp.float32
    )


def block_slot(row_block, col_block):
    return row_block * (row_block + 1) // 2 + col_block


def half_lower(square):
    size = square.shape[0]
    row_ids = lax.broadcasted_iota(jnp.int32, (size, size), 0)
    col_ids = lax.broadcasted_iota(jnp.int32, (size, size), 1)
    return jnp.where(row_ids > col_ids, square, jnp.where(row_ids == col_ids, 0.5 * square, 0.0))


def diagonal_adjoint(diagonal, inverse, lower_adj):
    inner = half_lower(inner_product(jnp.tril(diagonal), lower_adj))
    spread = inner_product(inverse, matmul(inner, inverse))
    return 0.5 * (spread + spread.T)


def rows_one(piece):
    return lax.all_gather(piece, "pcol", axis=1, tiled=True)


def owner_one(piece, root):
    return from_root(piece, "prow", root)


def reduce_one(term, count):
    return lax.psum_scatter(
        term(jnp.int32(0), lax.axis_size("pcol") * count), "pcol", scatter_dimension=0, tiled=True
    )


def trailing_product(trail, panels, gather_rows, send_owner, reduce_rows):
    prow_count = lax.axis_size("prow")
    pcol_count = lax.axis_size("pcol")
    cycles, sub_rows, width = panels.shape
    block = sub_rows * pcol_count
    gathered = gather_rows(panels[:, None]).reshape(cycles, block, width)
    column = lax.axis_index("pcol")
    col_cycles = trail.shape[3]
    global_block = 0 + column
    share = lax.dynamic_index_in_dim(gathered, global_block // prow_count, 0, keepdims=False)
    owned = [send_owner(share, global_block % prow_count)]
    stacked = jnp.stack(owned)
    view = trail.reshape(cycles, pcol_count, sub_rows, col_cycles, block)
    unit = cycles * sub_rows

    def term(start, count):
        product = jnp.einsum(
            "iaekb,kbn->aien", view, stacked, precision=HIGHEST, preferred_element_type=jnp.float32
        )
        return product.reshape(count, width)

    return reduce_rows(term, unit).reshape(cycles, sub_rows, width)


def per_device(adjoint_trail, factor_low, adjoint_low, factor_top, adjoint_top, diag_inverse):
    cycles = factor_low.shape[0]
    sub_rows = factor_low.shape[3]
    local_rows = cycles * sub_rows
    low_factor = factor_low.reshape(cycles, sub_rows, K * NB)
    low_adjoint = adjoint_low.reshape(local_rows, K, NB)
    columns = low_factor.reshape(local_rows, K, NB)
    top_factor, top_adjoint, inverses = (
        lax.all_gather(factor_top, "pcol", axis=1, tiled=True),
        lax.all_gather(adjoint_top, "pcol", axis=1, tiled=True),
        lax.all_gather(diag_inverse, "pcol", axis=1, tiled=True),
    )
    lower_grads = [None] * K
    diag_grads = [None] * K
    upper_grads = {}
    grams = {}

    def lower_step(panel):
        single = low_factor[:, :, panel * NB : (panel + 1) * NB]
        image = trailing_product(adjoint_trail, single, rows_one, owner_one, reduce_one).reshape(
            local_rows, NB
        )
        residual = low_adjoint[:, panel] - 2.0 * image
        for later in range(panel + 1, K):
            residual = residual - matmul(lower_grads[later], top_factor[block_slot(later, panel)])
        lower_grads[panel] = matmul(residual, inverses[panel])

    def top_step(panel):
        for row_block in range(panel + 1, K):
            top_residual = top_adjoint[block_slot(row_block, panel)] - grams[row_block, panel]
            top_residual = top_residual - 2.0 * matmul(
                diag_grads[row_block], top_factor[block_slot(row_block, panel)]
            )
            for middle in range(panel + 1, row_block):
                top_residual = top_residual - matmul(
                    upper_grads[middle, row_block], top_factor[block_slot(middle, panel)]
                )
            for beyond in range(row_block + 1, K):
                top_residual = top_residual - inner_product(
                    upper_grads[row_block, beyond], top_factor[block_slot(beyond, panel)]
                )
            upper_grads[panel, row_block] = matmul(top_residual, inverses[panel])
        lower_adj = top_adjoint[block_slot(panel, panel)] - grams[panel, panel]
        for row_block in range(panel + 1, K):
            lower_adj = lower_adj - inner_product(
                upper_grads[panel, row_block], top_factor[block_slot(row_block, panel)]
            )
        diag_grads[panel] = diagonal_adjoint(
            top_factor[block_slot(panel, panel)], inverses[panel], jnp.tril(lower_adj)
        )

    for panel in reversed(range(K)):
        lower_step(panel)
        local_gram = jnp.stack(
            [inner_product(lower_grads[panel], columns[:, earlier]) for earlier in range(panel + 1)]
        )
        summed = lax.psum(local_gram, ("prow", "pcol"))
        for earlier in range(panel + 1):
            grams[panel, earlier] = summed[earlier]
        top_step(panel)
    grad_low = jnp.stack(lower_grads, 1).reshape(factor_low.shape)
    blocks = []
    for row_block in range(K):
        for col_block in range(row_block + 1):
            if row_block == col_block:
                blocks.append(diag_grads[col_block])
            else:
                blocks.append(upper_grads[col_block, row_block])
    full_top = jnp.stack(blocks)
    share_rows = factor_top.shape[1]
    grad_top = lax.dynamic_slice_in_dim(
        full_top, lax.axis_index("pcol") * share_rows, share_rows, 1
    )
    return (grad_low, grad_top)


def solution(mesh):
    in_specs = (
        P(None, "prow", None, None, "pcol", None),
        P(None, "prow", "pcol", None, None, None),
        P(None, "prow", "pcol", None, None, None),
        P(None, "pcol", None),
        P(None, "pcol", None),
        P(None, "pcol", None),
    )
    out_specs = (P(None, "prow", "pcol", None, None, None), P(None, "pcol", None))
    return jax.shard_map(
        per_device, mesh=mesh, in_specs=in_specs, out_specs=out_specs, check_vma=False
    )
```

profile of v0, /device:TPU:8, one launch (start us, length us, event | category | flops | bytes accessed | tf_op | source)
XLA Modules:
  0.0 1294.8 jit_solution(6312719842912323253)
XLA Ops:
  9.0 37.8 %all-gather.3 = f32[2,256,256]{2,1,0:T(8,128)S(1)} all-gather(f32[2,8,256]{2,1,0:T(8,128)S(1)} %get-tuple-element.15), channel_id=5, replica_groups=mesh['prow'=16,'pcol'=32] {'pcol'}, dimensions={1}, use_global_device_ids=true | all-gather | bytes 540672 | tf_op jit(solution)/shard_map/all_gather | solution.py:44
  46.8 28.5 %all-gather.2 = f32[2,256,256]{2,1,0:T(8,128)S(1)} all-gather(f32[2,8,256]{2,1,0:T(8,128)S(1)} %get-tuple-element.16), channel_id=4, replica_groups=mesh['prow'=16,'pcol'=32] {'pcol'}, dimensions={1}, use_global_device_ids=true | all-gather | bytes 540672 | tf_op jit(solution)/shard_map/all_gather | solution.py:44
  76.7 29.8 %all-gather.1 = f32[2,256,256]{2,1,0:T(8,128)S(1)} all-gather(f32[2,8,256]{2,1,0:T(8,128)S(1)} %get-tuple-element.17), channel_id=3, replica_groups=mesh['prow'=16,'pcol'=32] {'pcol'}, dimensions={1}, use_global_device_ids=true | all-gather | bytes 540672 | tf_op jit(solution)/shard_map/all_gather | solution.py:44
  107.3 28.5 %all-gather = f32[2,256,256]{2,1,0:T(8,128)S(1)} all-gather(f32[2,8,256]{2,1,0:T(8,128)S(1)} %get-tuple-element.14), channel_id=2, replica_groups=mesh['prow'=16,'pcol'=32] {'pcol'}, dimensions={1}, use_global_device_ids=true | all-gather | bytes 540672 | tf_op jit(solution)/shard_map/all_gather | solution.py:44
  137.2 113.6 %all-reduce.7.cloned.1.call-done = (f32[256,256]{1,0:T(8,128)}, f32[256,256]{1,0:T(8,128)}, f32[256,256]{1,0:T(8,128)}, f32[256,256]{1,0:T(8,128)}) async-done(((f32[256,256]{1,0:T(8,128)}, f32[256,256]{1,0:T(8,128)}, f32[256,256]{1,0:T(8,128)}, f32[256,256]{1,0:T(8,128)}), (f32[256,256]{1,0:T(8,128)}, f32[256,256]{1,0:T(8,128)}, f32[256,256]{1,0:T(8,128)}, ...) | async-done | bytes 1048592 | tf_op jit(solution)/shard_map/psum | solution.py:13
  250.9 1.7 convolution_bitcast_fusion
  261.1 99.8 %reduce-scatter.11.cloned.1.call-done = f32[16,256]{1,0:T(8,128)} async-done(((f32[512,256]{1,0:T(8,128)}), f32[16,256]{1,0:T(8,128)}) %reduce-scatter.11.cloned.1.call-update) | async-done | bytes 16400 | tf_op jit(solution)/shard_map/reduce_scatter | solution.py:52
  364.8 104.2 %reduce-scatter.9.cloned.1.call-done = f32[16,256]{1,0:T(8,128)} async-done(((f32[512,256]{1,0:T(8,128)}), f32[16,256]{1,0:T(8,128)}) %reduce-scatter.9.cloned.1.call-update) | async-done | bytes 16400 | tf_op jit(solution)/shard_map/reduce_scatter | solution.py:52
  469.0 72.4 %all-gather.10.cloned.1.call-done = f32[10,256,256]{2,1,0:T(8,128)} async-done(((f32[10,8,256]{2,1,0:T(8,128)}), f32[10,256,256]{2,1,0:T(8,128)}) %all-gather.10.cloned.1.call-update) | async-done | bytes 2621456 | tf_op jit(solution)/shard_map/all_gather | solution.py:89
  541.4 1.3 convolution_subtract_fusion.19
  545.2 103.2 %reduce-scatter.7.cloned.1.call-done = f32[16,256]{1,0:T(8,128)} async-done(((f32[512,256]{1,0:T(8,128)}), f32[16,256]{1,0:T(8,128)}) %reduce-scatter.7.cloned.1.call-update) | async-done | bytes 16400 | tf_op jit(solution)/shard_map/reduce_scatter | solution.py:52
  648.4 1.2 convolution_subtract_fusion.18
  654.2 102.5 %reduce-scatter.5.cloned.1.call-done = f32[16,256]{1,0:T(8,128)} async-done(((f32[512,256]{1,0:T(8,128)}), f32[16,256]{1,0:T(8,128)}) %reduce-scatter.5.cloned.1.call-update) | async-done | bytes 16400 | tf_op jit(solution)/shard_map/reduce_scatter | solution.py:52
  760.5 1.9 pad_maximum_fusion.2
  764.3 65.2 %all-gather.12.cloned.1.call-done = f32[10,256,256]{2,1,0:T(8,128)} async-done(((f32[10,8,256]{2,1,0:T(8,128)}), f32[10,256,256]{2,1,0:T(8,128)}) %all-gather.12.cloned.1.call-update) | async-done | bytes 2621456 | tf_op jit(solution)/shard_map/all_gather | solution.py:90
  829.5 417.1 %all-reduce.5.cloned.1.call-done = (f32[2,256,256]{2,1,0:T(8,128)}, f32[3,256,256]{2,1,0:T(8,128)}, f32[4,256,256]{2,1,0:T(8,128)}, f32[1,256,256]{2,1,0:T(8,128)}) async-done(((f32[2,256,256]{2,1,0:T(8,128)}, f32[3,256,256]{2,1,0:T(8,128)}, f32[4,256,256]{2,1,0:T(8,128)}, f32[1,256,256]{2,1,0:T(8,128)}), (f32[2,256,256]{2,1,0:T(8,128)}, f32[3,256,256]{2,1,0:T(8,128)}, f32[4,256,256]{2,1,0:T(8,128)}, ...) | async-done | bytes 2621456 | tf_op jit(solution)/shard_map/psum | solution.py:137
  1246.6 1.5 fusion.18
  1248.1 1.3 fusion.62
  1249.5 1.5 fusion.66
  1251.2 1.5 fusion.8
  1252.7 1.3 fusion.69
  1254.0 1.6 fusion.7
  1258.0 1.5 fusion.5
  1260.0 1.3 fusion.72
  1261.3 1.5 fusion.6
  1264.8 1.6 convolution_subtract_fusion.11
  1267.9 1.3 fusion.71
  1269.2 1.8 copy.38
  1271.0 1.5 fusion.1
  1272.5 1.5 fusion.2
  1276.7 1.4 fusion.3
  1279.8 1.6 convolution_subtract_fusion.6
  (154 shorter events, 45.4 us)
Async XLA Ops:
  8.0 242.9 %all-reduce.7.cloned.1.call-start = ((), (), s32[]{:S(2)}) async-start(), calls=%async_computation.12 | async-start | bytes 2097152 | tf_op jit(solution)/shard_map/psum | solution.py:13
  9.0 128.2 %copy-start.19 = (f32[2,1,256,1,1,256]{5,4,3,2,1,0:T(1,128)S(1)}, f32[2,1,256,1,1,256]{5,4,3,2,1,0:T(1,128)}, u32[]{:S(2)}) copy-start(f32[2,1,256,1,1,256]{5,4,3,2,1,0:T(1,128)} %param.6) | copy-start | bytes 1572868
  136.6 124.5 %all-gather.8.cloned.1.call-start = ((), (), s32[]{:S(2)}) async-start(), calls=%async_computation.8 | async-start | bytes 1081344 | tf_op jit(solution)/shard_map/all_gather | solution.py:91
  137.1 223.8 %reduce-scatter.11.cloned.1.call-start = ((), (), s32[]{:S(2)}) async-start(), calls=%async_computation.7 | async-start | bytes 540672 | tf_op jit(solution)/shard_map/reduce_scatter | solution.py:52
  250.8 2.9 copy-start.25
  250.9 5.5 copy-start.24
  253.7 215.4 %reduce-scatter.9.cloned.1.call-start = ((), (), s32[]{:S(2)}) async-start(), calls=%async_computation.6 | async-start | bytes 540672 | tf_op jit(solution)/shard_map/reduce_scatter | solution.py:52
  253.7 4.6 copy-start.23
  255.6 285.9 %all-gather.10.cloned.1.call-start = ((), (), s32[]{:S(2)}) async-start(), calls=%async_computation.9 | async-start | bytes 2703360 | tf_op jit(solution)/shard_map/all_gather | solution.py:89
  256.3 392.1 %reduce-scatter.7.cloned.1.call-start = ((), (), s32[]{:S(2)}) async-start(), calls=%async_computation.5 | async-start | bytes 540672 | tf_op jit(solution)/shard_map/reduce_scatter | solution.py:52
  256.4 4.6 copy-start.27
  257.0 3.9 copy-start.26
  258.2 498.6 %reduce-scatter.5.cloned.1.call-start = ((), (), s32[]{:S(2)}) async-start(), calls=%async_computation.4 | async-start | bytes 540672 | tf_op jit(solution)/shard_map/reduce_scatter | solution.py:52
  260.1 569.4 %all-gather.12.cloned.1.call-start = ((), (), s32[]{:S(2)}) async-start(), calls=%async_computation.10 | async-start | bytes 2703360 | tf_op jit(solution)/shard_map/all_gather | solution.py:90
  260.7 985.9 %all-reduce.5.cloned.1.call-start = ((), (), s32[]{:S(2)}) async-start(), calls=%async_computation.11 | async-start | bytes 5242880 | tf_op jit(solution)/shard_map/psum | solution.py:137
  541.4 215.3 %copy-start = (f32[10,256,256]{2,1,0:T(8,128)S(1)}, f32[10,256,256]{2,1,0:T(8,128)}, u32[]{:S(2)}) copy-start(f32[10,256,256]{2,1,0:T(8,128)} %all-gather.10.cloned.1.call-done) | copy-start | bytes 7864324
  1251.1 5.0 copy-start.1
  1258.0 3.3 copy-start.11
  1258.0 5.4 copy-start.2
  1259.6 5.2 copy-start.20
  1261.3 5.7 copy-start.7
  1271.0 3.1 copy-start.8
  1271.0 3.9 copy-start.3
  1271.0 4.3 copy-start.5
  1275.2 6.8 copy-start.14
  1276.2 3.5 copy-start.22
  1276.7 4.7 copy-start.17
  1279.7 3.9 copy-start.13
  1283.2 3.3 copy-start.18
  1283.2 3.3 copy-start.6
  1283.2 3.3 copy-start.12
  1283.6 3.0 copy-start.15
  (5 other events, 9.8 us)
Sparse Core Ops, SparseCore 0:
  136.7 114.1 all-reduce.6
  763.6 482.9 all-reduce.4
Sparse Core Ops, SparseCore 1:
  139.2 67.6 all-gather.7
  253.7 107.1 reduce-scatter.10
  363.8 105.2 reduce-scatter.8
  471.2 70.2 all-gather.9
  544.2 104.1 reduce-scatter.6
  651.4 105.3 reduce-scatter.4
  758.8 70.6 all-gather.11
where the time goes:
time: 1300 us; the launch traced here: 1290 us
  waiting for transfers between devices  1080 us (83%)
  blocking collectives  125 us (10%)
  matrix products  53.2 us (4%)
  between operations  16.7 us (1%)
    psum x1, waiting for transfers between devices, per_device(): summed = lax.psum(local_gram, ('prow', 'pcol'))  417 us
    reduce_scatter x4, waiting for transfers between devices, reduce_one(): lax.psum_scatter(term(jnp.int32(0), lax.axis_size('pcol') * count), 'pcol...  410 us
    all_gather x4, blocking collectives, rows_one(): return lax.all_gather(piece, 'pcol', axis=1, tiled=True)  125 us
    psum x1, waiting for transfers between devices, from_root(): return lax.psum(jnp.where(mine, array, jnp.zeros_like(array)), axis)  114 us
    all_gather x1, waiting for transfers between devices, per_device(): lax.all_gather(factor_top, 'pcol', axis=1, tiled=True)  72.4 us
    all_gather x1, waiting for transfers between devices, per_device(): lax.all_gather(adjoint_top, 'pcol', axis=1, tiled=True)  65.2 us
    dot_general x30, matrix products, matmul(): jnp.dot(left, right, precision=HIGHEST, preferred_element_type=jnp.float32)  27.1 us
  transfers between devices with their start and end apart: 9, of which 8 were waited for; matrix products, arithmetic and copies ran while one was open for 2% of the time, Pallas kernels for 0%

commit v1 on v0

--- a/solution.py
+++ b/solution.py
@@ -134,7 +134,8 @@
         local_gram = jnp.stack(
             [inner_product(lower_grads[panel], columns[:, earlier]) for earlier in range(panel + 1)]
         )
-        summed = lax.psum(local_gram, ("prow", "pcol"))
+        half = lax.psum(local_gram, "prow")
+        summed = lax.psum(half, "pcol")
         for earlier in range(panel + 1):
             grams[panel, earlier] = summed[earlier]
         top_step(panel)

time: 1300 us -> 1150 us (0.88)
  the two profiles are of different devices: /device:TPU:8 before, /device:TPU:1 now
where the time goes in v1:
time: 1150 us
  waiting for transfers between devices  934 us (81%)
  blocking collectives  126 us (11%)
  matrix products  53.2 us (5%)
  between operations  16.7 us (1%)
    reduce_scatter x4, waiting for transfers between devices, reduce_one(): lax.psum_scatter(term(jnp.int32(0), lax.axis_size('pcol') * count), 'pcol...  405 us
    psum x1, waiting for transfers between devices, per_device(): summed = lax.psum(half, 'pcol')  216 us
    all_gather x4, blocking collectives, rows_one(): return lax.all_gather(piece, 'pcol', axis=1, tiled=True)  126 us
    psum x1, waiting for transfers between devices, per_device(): half = lax.psum(local_gram, 'prow')  123 us
    psum x1, waiting for transfers between devices, from_root(): return lax.psum(jnp.where(mine, array, jnp.zeros_like(array)), axis)  112 us
    all_gather x1, waiting for transfers between devices, per_device(): lax.all_gather(factor_top, 'pcol', axis=1, tiled=True)  76.1 us
    dot_general x30, matrix products, matmul(): jnp.dot(left, right, precision=HIGHEST, preferred_element_type=jnp.float32)  27.1 us
  transfers between devices with their start and end apart: 10, of which 8 were waited for; matrix products, arithmetic and copies ran while one was open for 2% of the time, Pallas kernels for 0%

profile of v1, /device:TPU:1, one launch (start us, length us, event | category | flops | bytes accessed | tf_op | source)
XLA Modules:
  0.0 1150.2 jit_solution(7169482205904475710)
XLA Ops:
  9.0 39.1 %all-gather.3 = f32[2,256,256]{2,1,0:T(8,128)S(1)} all-gather(f32[2,8,256]{2,1,0:T(8,128)S(1)} %get-tuple-element.19), channel_id=5, replica_groups=mesh['prow'=16,'pcol'=32] {'pcol'}, dimensions={1}, use_global_device_ids=true | all-gather | bytes 540672 | tf_op jit(solution)/shard_map/all_gather | solution.py:44
  48.1 28.5 %all-gather.2 = f32[2,256,256]{2,1,0:T(8,128)S(1)} all-gather(f32[2,8,256]{2,1,0:T(8,128)S(1)} %get-tuple-element.20), channel_id=4, replica_groups=mesh['prow'=16,'pcol'=32] {'pcol'}, dimensions={1}, use_global_device_ids=true | all-gather | bytes 540672 | tf_op jit(solution)/shard_map/all_gather | solution.py:44
  78.1 29.8 %all-gather.1 = f32[2,256,256]{2,1,0:T(8,128)S(1)} all-gather(f32[2,8,256]{2,1,0:T(8,128)S(1)} %get-tuple-element.21), channel_id=3, replica_groups=mesh['prow'=16,'pcol'=32] {'pcol'}, dimensions={1}, use_global_device_ids=true | all-gather | bytes 540672 | tf_op jit(solution)/shard_map/all_gather | solution.py:44
  108.6 28.5 %all-gather = f32[2,256,256]{2,1,0:T(8,128)S(1)} all-gather(f32[2,8,256]{2,1,0:T(8,128)S(1)} %get-tuple-element.18), channel_id=2, replica_groups=mesh['prow'=16,'pcol'=32] {'pcol'}, dimensions={1}, use_global_device_ids=true | all-gather | bytes 540672 | tf_op jit(solution)/shard_map/all_gather | solution.py:44
  138.5 112.3 %all-reduce.11.cloned.1.call-done = (f32[256,256]{1,0:T(8,128)}, f32[256,256]{1,0:T(8,128)}, f32[256,256]{1,0:T(8,128)}, f32[256,256]{1,0:T(8,128)}) async-done(((f32[256,256]{1,0:T(8,128)}, f32[256,256]{1,0:T(8,128)}, f32[256,256]{1,0:T(8,128)}, f32[256,256]{1,0:T(8,128)}), (f32[256,256]{1,0:T(8,128)}, f32[256,256]{1,0:T(8,128)}, f32[256,256]{1,0:T(8,128)}, ...) | async-done | bytes 1048592 | tf_op jit(solution)/shard_map/psum | solution.py:13
  250.8 1.7 convolution_bitcast_fusion
  260.2 98.6 %reduce-scatter.11.cloned.1.call-done = f32[16,256]{1,0:T(8,128)} async-done(((f32[512,256]{1,0:T(8,128)}), f32[16,256]{1,0:T(8,128)}) %reduce-scatter.11.cloned.1.call-update) | async-done | bytes 16400 | tf_op jit(solution)/shard_map/reduce_scatter | solution.py:52
  362.7 104.0 %reduce-scatter.9.cloned.1.call-done = f32[16,256]{1,0:T(8,128)} async-done(((f32[512,256]{1,0:T(8,128)}), f32[16,256]{1,0:T(8,128)}) %reduce-scatter.9.cloned.1.call-update) | async-done | bytes 16400 | tf_op jit(solution)/shard_map/reduce_scatter | solution.py:52
  466.7 76.1 %all-gather.10.cloned.1.call-done = f32[10,256,256]{2,1,0:T(8,128)} async-done(((f32[10,8,256]{2,1,0:T(8,128)}), f32[10,256,256]{2,1,0:T(8,128)}) %all-gather.10.cloned.1.call-update) | async-done | bytes 2621456 | tf_op jit(solution)/shard_map/all_gather | solution.py:89
  542.7 1.3 convolution_subtract_fusion.19
  546.5 100.2 %reduce-scatter.7.cloned.1.call-done = f32[16,256]{1,0:T(8,128)} async-done(((f32[512,256]{1,0:T(8,128)}), f32[16,256]{1,0:T(8,128)}) %reduce-scatter.7.cloned.1.call-update) | async-done | bytes 16400 | tf_op jit(solution)/shard_map/reduce_scatter | solution.py:52
  646.7 1.2 convolution_subtract_fusion.18
  652.5 102.3 %reduce-scatter.5.cloned.1.call-done = f32[16,256]{1,0:T(8,128)} async-done(((f32[512,256]{1,0:T(8,128)}), f32[16,256]{1,0:T(8,128)}) %reduce-scatter.5.cloned.1.call-update) | async-done | bytes 16400 | tf_op jit(solution)/shard_map/reduce_scatter | solution.py:52
  758.6 1.9 pad_maximum_fusion.2
  762.3 123.3 %all-reduce.9.cloned.1.call-done = (f32[2,256,256]{2,1,0:T(8,128)}, f32[3,256,256]{2,1,0:T(8,128)}, f32[4,256,256]{2,1,0:T(8,128)}, f32[1,256,256]{2,1,0:T(8,128)}) async-done(((f32[2,256,256]{2,1,0:T(8,128)}, f32[3,256,256]{2,1,0:T(8,128)}, f32[4,256,256]{2,1,0:T(8,128)}, f32[1,256,256]{2,1,0:T(8,128)}), (f32[2,256,256]{2,1,0:T(8,128)}, f32[3,256,256]{2,1,0:T(8,128)}, f32[4,256,256]{2,1,0:T(8,128)}, ...) | async-done | bytes 2621456 | tf_op jit(solution)/shard_map/psum | solution.py:137
  886.4 215.6 %all-reduce.7.cloned.1.call-done = (f32[2,256,256]{2,1,0:T(8,128)}, f32[3,256,256]{2,1,0:T(8,128)}, f32[4,256,256]{2,1,0:T(8,128)}, f32[1,256,256]{2,1,0:T(8,128)}) async-done(((f32[2,256,256]{2,1,0:T(8,128)}, f32[3,256,256]{2,1,0:T(8,128)}, f32[4,256,256]{2,1,0:T(8,128)}, f32[1,256,256]{2,1,0:T(8,128)}), (f32[2,256,256]{2,1,0:T(8,128)}, f32[3,256,256]{2,1,0:T(8,128)}, f32[4,256,256]{2,1,0:T(8,128)}, ...) | async-done | bytes 2621456 | tf_op jit(solution)/shard_map/psum | solution.py:138
  1102.0 1.5 fusion.18
  1103.5 1.3 fusion.62
  1104.8 1.5 fusion.66
  1106.6 1.5 fusion.8
  1108.1 1.3 fusion.69
  1109.4 1.6 fusion.7
  1113.4 1.5 fusion.5
  1115.3 1.3 fusion.72
  1116.7 1.5 fusion.6
  1119.9 1.6 convolution_subtract_fusion.11
  1123.0 1.3 fusion.71
  1124.4 1.8 copy.38
  1126.2 1.5 fusion.1
  1127.7 1.5 fusion.2
  1132.1 1.4 fusion.3
  1135.2 1.6 convolution_subtract_fusion.6
  (157 shorter events, 45.2 us)
Async XLA Ops:
  8.0 242.8 %all-reduce.11.cloned.1.call-start = ((), (), s32[]{:S(2)}) async-start(), calls=%async_computation.13 | async-start | bytes 2097152 | tf_op jit(solution)/shard_map/psum | solution.py:13
  9.0 129.5 %copy-start.19 = (f32[2,1,256,1,1,256]{5,4,3,2,1,0:T(1,128)S(1)}, f32[2,1,256,1,1,256]{5,4,3,2,1,0:T(1,128)}, u32[]{:S(2)}) copy-start(f32[2,1,256,1,1,256]{5,4,3,2,1,0:T(1,128)} %param.6) | copy-start | bytes 1572868
  137.9 122.3 %all-gather.8.cloned.1.call-start = ((), (), s32[]{:S(2)}) async-start(), calls=%async_computation.8 | async-start | bytes 1081344 | tf_op jit(solution)/shard_map/all_gather | solution.py:91
  138.4 220.4 %reduce-scatter.11.cloned.1.call-start = ((), (), s32[]{:S(2)}) async-start(), calls=%async_computation.7 | async-start | bytes 540672 | tf_op jit(solution)/shard_map/reduce_scatter | solution.py:52
  250.8 5.5 copy-start.24
  253.6 213.1 %reduce-scatter.9.cloned.1.call-start = ((), (), s32[]{:S(2)}) async-start(), calls=%async_computation.6 | async-start | bytes 540672 | tf_op jit(solution)/shard_map/reduce_scatter | solution.py:52
  253.7 4.5 copy-start.27
  254.3 3.9 copy-start.26
  254.4 3.9 copy-start.23
  255.5 287.2 %all-gather.10.cloned.1.call-start = ((), (), s32[]{:S(2)}) async-start(), calls=%async_computation.9 | async-start | bytes 2703360 | tf_op jit(solution)/shard_map/all_gather | solution.py:89
  256.3 390.4 %reduce-scatter.7.cloned.1.call-start = ((), (), s32[]{:S(2)}) async-start(), calls=%async_computation.5 | async-start | bytes 540672 | tf_op jit(solution)/shard_map/reduce_scatter | solution.py:52
  258.1 496.7 %reduce-scatter.5.cloned.1.call-start = ((), (), s32[]{:S(2)}) async-start(), calls=%async_computation.4 | async-start | bytes 540672 | tf_op jit(solution)/shard_map/reduce_scatter | solution.py:52
  260.1 625.5 %all-reduce.9.cloned.1.call-start = ((), (), s32[]{:S(2)}) async-start(), calls=%async_computation.12 | async-start | bytes 5242880 | tf_op jit(solution)/shard_map/psum | solution.py:137
  542.7 212.1 %copy-start = (f32[10,256,256]{2,1,0:T(8,128)S(1)}, f32[10,256,256]{2,1,0:T(8,128)}, u32[]{:S(2)}) copy-start(f32[10,256,256]{2,1,0:T(8,128)} %all-gather.10.cloned.1.call-done) | copy-start | bytes 7864324
  761.5 124.9 %all-gather.12.cloned.1.call-start = ((), (), s32[]{:S(2)}) async-start(), calls=%async_computation.10 | async-start | bytes 2703360 | tf_op jit(solution)/shard_map/all_gather | solution.py:90
  762.1 339.9 %all-reduce.7.cloned.1.call-start = ((), (), s32[]{:S(2)}) async-start(), calls=%async_computation.11 | async-start | bytes 5242880 | tf_op jit(solution)/shard_map/psum | solution.py:138
  1106.5 5.0 copy-start.1
  1113.4 3.3 copy-start.11
  1113.4 5.4 copy-start.2
  1114.9 5.0 copy-start.20
  1116.7 5.4 copy-start.7
  1126.2 3.1 copy-start.8
  1126.2 3.9 copy-start.3
  1126.2 4.3 copy-start.5
  1130.5 7.0 copy-start.14
  1131.7 3.5 copy-start.22
  1132.1 4.7 copy-start.17
  1135.2 3.9 copy-start.13
  1138.6 3.3 copy-start.18
  1138.6 3.3 copy-start.6
  1138.6 3.3 copy-start.12
  1139.0 3.0 copy-start.15
  (6 other events, 13.3 us)
Sparse Core Ops, SparseCore 0:
  138.0 112.7 all-reduce.10
  761.6 123.9 all-reduce.8
Sparse Core Ops, SparseCore 1:
  140.5 67.5 all-gather.7
  253.7 105.0 reduce-scatter.10
  361.7 104.9 reduce-scatter.8
  468.8 73.8 all-gather.9
  545.5 101.1 reduce-scatter.6
  649.7 105.1 reduce-scatter.4
  764.1 73.4 all-gather.11
  885.7 216.2 all-reduce.6
